TPU v7x, 128 devices: a whole 4x4x4 slice. The times are simulated.
128 devices in a mesh: blk: 32 (over x, y_hi, z), grp: 4 (over y_lo, core).
Axes of the slice: x: 4, y: 4 (y_hi: 2, y_lo: 2; y = y_hi * 2 + y_lo), z: 4, core: 2. Of those that a mesh axis runs over, the one named last changes fastest.
Arguments:
- amplitudes: bfloat16 [1920, 1920], P('blk'), may hold values from -6 to 6
- hole_panel: bfloat16 [1920, 32, 1920], P(None, 'blk', 'grp'), may hold values from -0.375 to 0.375
- virt_fock: bfloat16 [1920, 1920], replicated, may hold values from -0.125 to 0.125
- irrep_sizes: int32 [8], replicated, may hold values from 1 to 480, 1920 in all
- pair_irreps: int32 [32], P('blk'), may hold values from 0 to 7
Outputs:
- dressed: bfloat16 [1920, 32, 1920], P('grp', 'blk')
Inputs may be any that keep to these rules, and one draw needn't show every extreme that they name: `irrep_sizes`: the 8 entries sum to 1920.
All inputs are finite; a program needn't handle non-finite values.
Results may differ from a plain program's by a relative error of at most 0.0049.
Values may be sent and summed in bfloat16 or wider, within the bound.
A program may use at most 128 MiB of HBM per device.

v0:
```python
import jax
import jax.numpy as jnp
from jax import lax
from jax.sharding import PartitionSpec as P


def irrep_of(positions, block_sizes):
    bounds = jnp.cumsum(block_sizes)[:-1]
    return jnp.sum((positions[:, None] >= bounds[None, :]).astype(jnp.int32), axis=1)


def make_local(n_blk, n_grp):

    def local(amplitudes, hole_panel, virt_fock, irrep_sizes, pair_irreps):
        rows = amplitudes.shape[0]
        virtuals = amplitudes.shape[1]
        quarter = hole_panel.shape[2]
        g = lax.axis_index("grp")
        piece = rows // n_grp
        per = n_blk // n_grp
        perm = []
        for q in range(n_grp):
            for k in range(per):
                for i in range(n_grp):
                    perm.append(((per * q + k) * n_grp + i, (n_grp * k + i) * n_grp + q))
        mine = lax.dynamic_slice_in_dim(amplitudes, g * piece, piece, 0)
        mine = lax.ppermute(mine, ("blk", "grp"), perm)
        t_rows = lax.all_gather(mine, "blk", axis=0, tiled=True)
        labels = irrep_of(jnp.arange(virtuals, dtype=jnp.int32), irrep_sizes)
        panel = lax.all_gather(hole_panel.reshape(virtuals, quarter), "grp", axis=1, tiled=True)
        allowed = jnp.bitwise_xor(labels[:, None], labels[None, :]) == pair_irreps[0]
        masked = jnp.where(allowed, panel, jnp.zeros((), jnp.bfloat16))
        coupled = jnp.dot(t_rows, masked, preferred_element_type=jnp.float32).astype(jnp.bfloat16)
        out = jnp.dot(coupled, virt_fock, preferred_element_type=jnp.float32).astype(jnp.bfloat16)
        return out.reshape(quarter, 1, virtuals)

    return local


def solution(mesh):
    in_specs = (P("blk", None), P(None, "blk", "grp"), P(), P(), P("blk"))
    out_specs = P("grp", "blk", None)
    local = make_local(mesh.shape["blk"], mesh.shape["grp"])
    return jax.shard_map(local, mesh=mesh, in_specs=in_specs, out_specs=out_specs, check_vma=False)
```

profile of v0, /device:TPU:1, one launch (start us, length us, event | category | flops | bytes accessed | tf_op | source)
XLA Modules:
  0.0 186.1 jit_solution(730050720383567158)
XLA Ops:
  6.5 0.0 copy-start
  6.5 0.0 all-gather.7.cloned.1.call-start
  6.5 0.9 copy-done
  7.5 4.9 %collective-permute-start = (bf16[15,1920]{1,0:T(8,128)(2,1)S(1)}, bf16[15,1920]{1,0:T(8,128)(2,1)S(1)}, u32[]{:S(2)}, u32[]{:S(2)}) collective-permute-start(bf16[15,1920]{1,0:T(8,128)(2,1)S(1)} %constant_dynamic-slice_fusion), channel_id=1, source_target_pairs={{0,0},{1,4},{2,8},{3,12},{4,16},{5,20},{6,24},{7,28},{8,32},{9,36}... | collective-permute-start | bytes 172808 | tf_op jit(solution)/shard_map/ppermute | solution.py:27
  12.4 1.8 collective-permute-done
  14.3 0.0 copy-start.1
  14.3 0.6 copy-done.1
  14.9 0.0 all-gather.7.cloned.1.call-update
  14.9 0.0 all-gather.5.cloned.1.call-start
  14.9 0.7 all-gather.5.cloned.1.call-update
  15.7 0.8 reduce-window.4
  17.1 0.1 convert_reduce_fusion
  17.2 73.9 %all-gather.7.cloned.1.call-done = bf16[32,15,1920]{2,1,0:T(8,128)(2,1)} async-done(((bf16[1,15,1920]{2,1,0:T(8,128)(2,1)}), bf16[32,15,1920]{2,1,0:T(8,128)(2,1)}) %all-gather.7.cloned.1.call-update) | async-done | bytes 1843216 | tf_op jit(solution)/shard_map/all_gather | solution.py:28
  91.2 1.8 reshape.20
  93.0 71.4 %all-gather.5.cloned.1.call-done = bf16[1920,1,1920]{0,2,1:T(8,128)(2,1)} async-done(((bf16[1920,1,480]{0,2,1:T(8,128)(2,1)}), bf16[1920,1,1920]{0,2,1:T(8,128)(2,1)}) %all-gather.5.cloned.1.call-update) | async-done | bytes 7372816 | tf_op jit(solution)/shard_map/all_gather | solution.py:30
  164.4 14.8 %fusion.11 = bf16[480,1,1920]{2,0,1:T(8,128)(2,1)} fusion(bf16[1920,1920]{1,0:T(8,128)(2,1)} %param.7, bf16[480,1920]{1,0:T(8,128)(2,1)S(1)} %reshape.20, bf16[1920,1,1920]{0,2,1:T(8,128)(2,1)} %all-gather.5.cloned.1.call-done, s32[]{:T(128)} %bitcast.25, s32[1920]{0:T(1024)S(1)} %convert_reduce_fusion), kind=kOutput, calls=%fused_computation.10 | convolution fusion | flops 7090790400 | bytes 18439684 | tf_op jit(solution)/shard_map/dot_general | solution.py:34
  (2 shorter events, 0.0 us)
Async XLA Ops:
  6.5 0.9 copy-start
  6.5 84.6 %all-gather.7.cloned.1.call-start = ((), (), s32[]{:S(2)}) async-start(), calls=%async_computation.1 | async-start | bytes 2027520 | tf_op jit(solution)/shard_map/all_gather | solution.py:28
  7.5 6.7 %collective-permute-start = (bf16[15,1920]{1,0:T(8,128)(2,1)S(1)}, bf16[15,1920]{1,0:T(8,128)(2,1)S(1)}, u32[]{:S(2)}, u32[]{:S(2)}) collective-permute-start(bf16[15,1920]{1,0:T(8,128)(2,1)S(1)} %constant_dynamic-slice_fusion), channel_id=1, source_target_pairs={{0,0},{1,4},{2,8},{3,12},{4,16},{5,20},{6,24},{7,28},{8,32},{9,36}... | collective-permute-start | bytes 172808 | tf_op jit(solution)/shard_map/ppermute | solution.py:27
  14.3 0.6 copy-start.1
  14.9 149.5 %all-gather.5.cloned.1.call-start = ((), (), s32[]{:S(2)}) async-start(), calls=%async_computation | async-start | bytes 9216000 | tf_op jit(solution)/shard_map/all_gather | solution.py:30
Sparse Core Ops, SparseCore 0:
  15.0 76.1 all-gather.6
  92.8 71.5 all-gather.4
where the time goes:
time: 186 us
  waiting for transfers between devices  148 us (80%)
  matrix products  14.8 us (8%)
  between operations  14.1 us (8%)
  starting transfers between devices  4.98 us (3%)
  local copies, waits for them, and re-layouts  3.4 us (2%)
    all_gather x1, waiting for transfers between devices, local(): t_rows = lax.all_gather(mine, 'blk', axis=0, tiled=True)  73.9 us
    all_gather x1, waiting for transfers between devices, local(): lax.all_gather(hole_panel.reshape(virtuals, quarter), 'grp', axis=1, tile...  71.4 us
    dot_general x1, matrix products, local(): jnp.dot(coupled, virt_fock, preferred_element_type=jnp.float32)  14.8 us
    ppermute x1, starting transfers between devices, local(): mine = lax.ppermute(mine, ('blk', 'grp'), perm)  4.94 us
  transfers between devices with their start and end apart: 3, of which 3 were waited for; matrix products, arithmetic and copies ran while one was open for 1% of the time, Pallas kernels for 0%

commit v1 on v0

--- a/solution.py
+++ b/solution.py
@@ -25,7 +25,9 @@
                     perm.append(((per * q + k) * n_grp + i, (n_grp * k + i) * n_grp + q))
         mine = lax.dynamic_slice_in_dim(amplitudes, g * piece, piece, 0)
         mine = lax.ppermute(mine, ("blk", "grp"), perm)
-        t_rows = lax.all_gather(mine, "blk", axis=0, tiled=True)
+        t_rows = jnp.concatenate(
+            lax.all_to_all(jnp.stack([mine] * lax.axis_size("blk")), "blk", 0, 0), axis=0
+        )
         labels = irrep_of(jnp.arange(virtuals, dtype=jnp.int32), irrep_sizes)
         panel = lax.all_gather(hole_panel.reshape(virtuals, quarter), "grp", axis=1, tiled=True)
         allowed = jnp.bitwise_xor(labels[:, None], labels[None, :]) == pair_irreps[0]

time: 186 us -> 129 us (0.69)
  waiting for transfers between devices: 148 us -> 77.4 us
  starting transfers between devices: 4.98 us -> 18.5 us
    all_gather x1 -> x0, waiting for transfers between devices: 73.9 us -> none  [local(): t_rows = lax.all_gather(mine, 'blk', axis=0, tiled=True)]
    all_to_all x0 -> x1, waiting for transfers between devices: none -> 30.8 us  [local(): lax.all_to_all(jnp.stack([mine] * lax.axis_size('blk')), 'blk', 0, 0)]
    all_gather x1, waiting for transfers between devices: 71.4 us -> 44.1 us  [local(): lax.all_gather(hole_panel.reshape(virtuals, quarter), 'grp', axis=1, tile...]
    all_to_all x0 -> x1, starting transfers between devices: none -> 13.5 us  [local(): lax.all_to_all(jnp.stack([mine] * lax.axis_size('blk')), 'blk', 0, 0)]
    unnamed x5 -> x4, local copies, waits for them, and re-layouts: 3.37 us -> 0.22 us
  transfers between devices with their start and end apart: 3 -> 3, of which waited for: 3 -> 3; matrix products, arithmetic and copies ran while one was open for 1% -> 3% of each run, Pallas kernels for 0% -> 0%
where the time goes in v1:
time: 129 us
  waiting for transfers between devices  77.4 us (60%)
  starting transfers between devices  18.5 us (14%)
  matrix products  15.3 us (12%)
  between operations  14.1 us (11%)
  local copies, waits for them, and re-layouts  3.32 us (3%)
    all_gather x1, waiting for transfers between devices, local(): lax.all_gather(hole_panel.reshape(virtuals, quarter), 'grp', axis=1, tile...  44.1 us
    all_to_all x1, waiting for transfers between devices, local(): lax.all_to_all(jnp.stack([mine] * lax.axis_size('blk')), 'blk', 0, 0)  30.8 us
    dot_general x1, matrix products, local(): jnp.dot(coupled, virt_fock, preferred_element_type=jnp.float32)  15.3 us
    all_to_all x1, starting transfers between devices, local(): lax.all_to_all(jnp.stack([mine] * lax.axis_size('blk')), 'blk', 0, 0)  13.5 us
    ppermute x1, starting transfers between devices, local(): mine = lax.ppermute(mine, ('blk', 'grp'), perm)  4.94 us
  transfers between devices with their start and end apart: 3, of which 3 were waited for; matrix products, arithmetic and copies ran while one was open for 3% of the time, Pallas kernels for 0%

profile of v1, /device:TPU:1, one launch (start us, length us, event | category | flops | bytes accessed | tf_op | source)
XLA Modules:
  0.0 128.8 jit_solution(4137564691364419771)
XLA Ops:
  6.5 0.0 copy-start
  6.5 0.0 copy-start.1
  6.5 0.0 all-gather.3.cloned.1.call-start
  6.5 0.7 all-gather.3.cloned.1.call-update
  7.3 0.2 copy-done
  7.5 4.9 %collective-permute-start = (bf16[15,1920]{1,0:T(8,128)(2,1)S(1)}, bf16[15,1920]{1,0:T(8,128)(2,1)S(1)}, u32[]{:S(2)}, u32[]{:S(2)}) collective-permute-start(bf16[15,1920]{1,0:T(8,128)(2,1)S(1)} %constant_dynamic-slice_fusion), channel_id=1, source_target_pairs={{0,0},{1,4},{2,8},{3,12},{4,16},{5,20},{6,24},{7,28},{8,32},{9,36}... | collective-permute-start | bytes 172808 | tf_op jit(solution)/shard_map/ppermute | solution.py:27
  12.4 1.8 %collective-permute-done = bf16[15,1920]{1,0:T(8,128)(2,1)S(1)} collective-permute-done((bf16[15,1920]{1,0:T(8,128)(2,1)S(1)}, bf16[15,1920]{1,0:T(8,128)(2,1)S(1)}, u32[]{:S(2)}, u32[]{:S(2)}) %collective-permute-start) | collective-permute-done | bytes 57632 | tf_op jit(solution)/shard_map/ppermute | solution.py:27
  14.3 1.5 %stack.2 = bf16[32,15,1920]{2,1,0:T(8,128)(2,1)} broadcast(bf16[15,1920]{1,0:T(8,128)(2,1)S(1)} %collective-permute-done), dimensions={1,2} | broadcast | bytes 1900800 | tf_op jit(solution)/shard_map/stack | solution.py:29
  15.7 13.5 %all-to-all-start = ((bf16[32,15,1920]{2,1,0:T(8,128)(2,1)}), bf16[32,15,1920]{2,1,0:T(8,128)(2,1)S(1)}, u32[]{:S(2)}, u32[]{:S(2)}) async-start(bf16[32,15,1920]{2,1,0:T(8,128)(2,1)} %stack.2), calls=%async_computation | async-start | bytes 3932160 | tf_op jit(solution)/shard_map/all_to_all | solution.py:29
  29.3 0.0 copy-done.1
  29.3 0.2 reduce-window.4
  30.1 0.1 convert_reduce_fusion
  30.2 30.8 %all-to-all-done = bf16[32,15,1920]{2,1,0:T(8,128)(2,1)S(1)} async-done(((bf16[32,15,1920]{2,1,0:T(8,128)(2,1)}), bf16[32,15,1920]{2,1,0:T(8,128)(2,1)S(1)}, u32[]{:S(2)}, u32[]{:S(2)}) %all-to-all-start) | async-done | bytes 1843232 | tf_op jit(solution)/shard_map/all_to_all | solution.py:29
  61.0 1.6 %reshape.20 = bf16[480,1920]{1,0:T(8,128)(2,1)} reshape(bf16[32,15,1920]{2,1,0:T(8,128)(2,1)S(1)} %all-to-all-done) | data formatting | bytes 3686400 | tf_op jit(solution)/shard_map/reshape | solution.py:28
  62.6 44.1 %all-gather.3.cloned.1.call-done = bf16[1920,1,1920]{0,2,1:T(8,128)(2,1)} async-done(((bf16[1920,1,480]{0,2,1:T(8,128)(2,1)}), bf16[1920,1,1920]{0,2,1:T(8,128)(2,1)}) %all-gather.3.cloned.1.call-update) | async-done | bytes 7372816 | tf_op jit(solution)/shard_map/all_gather | solution.py:32
  106.7 15.3 %fusion.11 = bf16[480,1,1920]{2,0,1:T(8,128)(2,1)} fusion(bf16[1920,1920]{1,0:T(8,128)(2,1)} %param.7, bf16[480,1920]{1,0:T(8,128)(2,1)} %reshape.20, bf16[1920,1,1920]{0,2,1:T(8,128)(2,1)} %all-gather.3.cloned.1.call-done, s32[]{:T(128)} %bitcast.24, s32[1920]{0:T(1024)S(1)} %convert_reduce_fusion), kind=kOutput, calls=%fused_computation.10 | convolution fusion | flops 7090790400 | bytes 18439684 | tf_op jit(solution)/shard_map/dot_general | solution.py:36
  (2 shorter events, 0.0 us)
Async XLA Ops:
  6.5 0.9 copy-start
  6.5 22.7 %copy-start.1 = (s32[8]{0:T(128)S(1)}, s32[8]{0:T(128)}, u32[]{:S(2)}) copy-start(s32[8]{0:T(128)} %param.8) | copy-start | bytes 100
  6.5 100.2 %all-gather.3.cloned.1.call-start = ((), (), s32[]{:S(2)}) async-start(), calls=%async_computation.1 | async-start | bytes 9216000 | tf_op jit(solution)/shard_map/all_gather | solution.py:32
  7.5 6.7 %collective-permute-start = (bf16[15,1920]{1,0:T(8,128)(2,1)S(1)}, bf16[15,1920]{1,0:T(8,128)(2,1)S(1)}, u32[]{:S(2)}, u32[]{:S(2)}) collective-permute-start(bf16[15,1920]{1,0:T(8,128)(2,1)S(1)} %constant_dynamic-slice_fusion), channel_id=1, source_target_pairs={{0,0},{1,4},{2,8},{3,12},{4,16},{5,20},{6,24},{7,28},{8,32},{9,36}... | collective-permute-start | bytes 172808 | tf_op jit(solution)/shard_map/ppermute | solution.py:27
  15.7 45.3 %all-to-all-start = ((bf16[32,15,1920]{2,1,0:T(8,128)(2,1)}), bf16[32,15,1920]{2,1,0:T(8,128)(2,1)S(1)}, u32[]{:S(2)}, u32[]{:S(2)}) async-start(bf16[32,15,1920]{2,1,0:T(8,128)(2,1)} %stack.2), calls=%async_computation | async-start | bytes 3932160 | tf_op jit(solution)/shard_map/all_to_all | solution.py:29
Sparse Core Ops, SparseCore 0:
  9.0 97.6 all-gather.2
